TPU v7x, 256 devices: a whole 4x4x8 slice. The times are simulated.
256 devices in a mesh: grp: 8 (over z_hi, y), row: 32 (over z_lo, x, core).
Axes of the slice: x: 4, y: 4, z: 8 (z_hi: 2, z_lo: 4; z = z_hi * 4 + z_lo), core: 2. Of those that a mesh axis runs over, the one named last changes fastest.
Arguments:
- points: bfloat16 [524288, 128], P(('grp', 'row')), as said below
- centers: bfloat16 [8192, 128], replicated, as said below
- inner_factor: bfloat16 [8192, 8192], P('row'), as said below
- outer_factor: bfloat16 [8192, 8192], P('row'), as said below
- iterate: float32 [64, 8192], P(None, 'row'), may hold values from -6 to 6
- residual: float32 [64, 8192], P(None, 'row'), as said below
- direction: float32 [64, 8192], P(None, 'row'), as said below
Outputs:
- next_iterate: float32 [64, 8192], P(None, 'row')
- next_residual: float32 [64, 8192], P(None, 'row')
- next_direction: float32 [64, 8192], P(None, 'row')
Inputs may be any that keep to these rules, and one draw needn't show every extreme that they name: `inner_factor`: upper triangular: zero below the diagonal, positive on it. `outer_factor`: upper triangular: zero below the diagonal, positive on it. `residual`: finite real values. `direction`: finite real values. `points`: finite real values. `centers`: finite real values.
All inputs are finite; a program needn't handle non-finite values.
Results may differ from a plain program's by a relative error of at most 0.0056.
Values may be sent and summed in bfloat16 or wider, within the bound.
No kernel may reach another device: no remote copies, remote signals or barrier semaphores. Data moves between devices by JAX's collectives and lax.ppermute only.
A program may use at most 64 MiB of HBM per device.

v0:
```python
import jax
import jax.numpy as jnp
from jax import lax
from jax.sharding import PartitionSpec as P

ridge_weight = 0.5


def kernel_rows(block_points, centers, center_norms):
    point_wide = block_points.astype(jnp.float32)
    point_norms = jnp.sum(point_wide * point_wide, axis=1)
    cross_term = lax.dot_general(
        block_points, centers, (((1,), (1,)), ((), ())), preferred_element_type=jnp.float32
    )
    distance = point_norms[:, None] + center_norms[None, :] - 2.0 * cross_term
    return jnp.exp(distance * (-4.0 / block_points.shape[1])).astype(jnp.bfloat16)


def local(points, centers, inner_factor, outer_factor, iterate, residual, direction):
    contract_last = (((1,), (1,)), ((), ()))
    own_rows = inner_factor.shape[0]
    targets = direction.shape[0]
    direction_half = direction.astype(jnp.bfloat16)
    columns = inner_factor
    inner_term = lax.dot_general(
        lax.all_gather(direction_half, "row", axis=1, tiled=True),
        columns,
        contract_last,
        preferred_element_type=jnp.float32,
    )
    inner_half = inner_term.astype(jnp.bfloat16)
    columns = outer_factor
    outer_rows = lax.dot_general(
        lax.all_gather(inner_half, "row", axis=1, tiled=True),
        columns,
        contract_last,
        preferred_element_type=jnp.float32,
    )
    outer_half = lax.all_gather(outer_rows.astype(jnp.bfloat16), "row", axis=1, tiled=True)
    center_wide = centers.astype(jnp.float32)
    center_norms = jnp.sum(center_wide * center_wide, axis=1)
    local_points = points.shape[0]
    block_rows = min(512, local_points)
    point_blocks = points.reshape(local_points // block_rows, block_rows, points.shape[1])

    def one_block(carried, block_points):
        kernel_block = kernel_rows(block_points, centers, center_norms)
        fitted = lax.dot_general(
            outer_half, kernel_block, contract_last, preferred_element_type=jnp.float32
        ).astype(jnp.bfloat16)
        return (carried + jnp.dot(fitted, kernel_block, preferred_element_type=jnp.float32), None)

    partial_sums, _ = lax.scan(
        one_block, jnp.zeros((targets, centers.shape[0]), jnp.float32), point_blocks
    )
    summed_all = lax.psum(partial_sums, ("grp", "row"))
    own_normal = lax.dynamic_slice_in_dim(summed_all, lax.axis_index("row") * own_rows, own_rows, 1)
    normal_half = own_normal.astype(jnp.bfloat16)
    point_count = local_points * lax.axis_size("grp") * lax.axis_size("row")
    outer_terms = jnp.dot(normal_half, outer_factor, preferred_element_type=jnp.float32)
    shaped = (
        lax.psum_scatter(outer_terms, "row", scatter_dimension=1, tiled=True) / point_count
        + ridge_weight * inner_term
    )
    shaped_half = shaped.astype(jnp.bfloat16)
    inner_terms = jnp.dot(shaped_half, inner_factor, preferred_element_type=jnp.float32)
    operator_image = lax.psum_scatter(inner_terms, "row", scatter_dimension=1, tiled=True)
    old_norm = lax.psum(jnp.sum(residual * residual, axis=1), "row")
    curvature = lax.psum(jnp.sum(direction * operator_image, axis=1), "row")
    step_size = old_norm / curvature
    next_residual = residual - step_size[:, None] * operator_image
    new_norm = lax.psum(jnp.sum(next_residual * next_residual, axis=1), "row")
    next_iterate = iterate + step_size[:, None] * direction
    next_direction = next_residual + (new_norm / old_norm)[:, None] * direction
    return (next_iterate, next_residual, next_direction)


def solution(mesh):
    placed = (
        P(("grp", "row"), None),
        P(),
        P("row", None),
        P("row", None),
        P(None, "row"),
        P(None, "row"),
        P(None, "row"),
    )
    return jax.shard_map(
        local,
        mesh=mesh,
        in_specs=placed,
        out_specs=(P(None, "row"), P(None, "row"), P(None, "row")),
        check_vma=False,
    )
```

profile of v0, /device:TPU:1, one launch (start us, length us, event | category | flops | bytes accessed | tf_op | source)
XLA Modules:
  0.0 819.4 jit_solution(775019206389307324)
XLA Ops:
  7.2 1.5 convert_element_type.29
  8.7 66.0 %all-gather.4.cloned.1.call-done = bf16[64,8192]{1,0:T(8,128)(2,1)} async-done(((bf16[64,256]{1,0:T(8,128)(2,1)}), bf16[64,8192]{1,0:T(8,128)(2,1)}) %all-gather.4.cloned.1.call-update) | async-done | bytes 1048592 | tf_op jit(solution)/shard_map/all_gather | solution.py:26
  74.8 4.5 fusion.10
  79.4 59.4 %all-gather.6.cloned.1.call-done = bf16[64,8192]{1,0:T(8,128)(2,1)} async-done(((bf16[64,256]{1,0:T(8,128)(2,1)}), bf16[64,8192]{1,0:T(8,128)(2,1)}) %all-gather.6.cloned.1.call-update) | async-done | bytes 1048592 | tf_op jit(solution)/shard_map/all_gather | solution.py:34
  138.7 4.5 convolution_convert_fusion.1
  143.5 2.7 multiply_reduce_fusion.1
  146.3 56.4 %all-gather.8.cloned.1.call-done = bf16[64,8192]{1,0:T(8,128)(2,1)} async-done(((bf16[64,256]{1,0:T(8,128)(2,1)}), bf16[64,8192]{1,0:T(8,128)(2,1)}) %all-gather.8.cloned.1.call-update) | async-done | bytes 1048592 | tf_op jit(solution)/shard_map/all_gather | solution.py:39
  202.7 87.9 %while.11 = (s32[]{:T(128)}, f32[64,8192]{1,0:T(8,128)S(1)}, bf16[4,512,128]{2,1,0:T(8,128)(2,1)}, f32[8192]{0:T(1024)S(1)}, bf16[8192,128]{1,0:T(8,128)(2,1)}, ...) while((s32[]{:T(128)}, f32[64,8192]{1,0:T(8,128)S(1)}, bf16[4,512,128]{2,1,0:T(8,128)(2,1)}, ...), condition=%wide.region_5.6_spmd.clone, body=%wide.region_3.0_spmd.clone.sunk | while | flops 2169732608 | bytes 28610700 | solution.py:53
  203.7 9.0 %exponential_convert_fusion.2 = bf16[512,8192]{1,0:T(8,128)(2,1)} fusion(bf16[8192,128]{1,0:T(8,128)(2,1)} %get-tuple-element.134, f32[8192]{0:T(1024)S(1)} %get-tuple-element.133, f32[512]{0:T(512)S(1)} %multiply_reduce_fusion.6, bf16[4,512,128]{2,1,0:T(8,128)(2,1)} %get-tuple-element.132, s32[]{:T(128)S(6)} %copy.12), kind=kOutput, calls=%fused_computation.clone.1 | convolution fusion | flops 1094713344 | bytes 10651652 | tf_op jit(solution)/shard_map/while/body/eval_jaxpr/dot_general | solution.py:12
  212.8 11.9 %convolution_add_fusion.2 = f32[64,8192]{1,0:T(8,128)S(1)} fusion(bf16[512,8192]{1,0:T(8,128)(2,1)} %exponential_convert_fusion.2, f32[64,8192]{1,0:T(8,128)S(1)} %get-tuple-element.123, pred[]{:T(512)S(6)} %compare.3, bf16[64,8192]{1,0:T(8,128)(2,1)S(1)} %copy-done), kind=kOutput, calls=%fused_computation.1.clone.1 | convolution fusion | flops 1074823168 | bytes 13631489 | tf_op jit(solution)/shard_map/while/body/eval_jaxpr/dot_general | solution.py:51
  224.7 1.1 multiply_reduce_fusion.6
  225.7 9.0 %exponential_convert_fusion.2 = bf16[512,8192]{1,0:T(8,128)(2,1)} fusion(bf16[8192,128]{1,0:T(8,128)(2,1)} %get-tuple-element.134, f32[8192]{0:T(1024)S(1)} %get-tuple-element.133, f32[512]{0:T(512)S(1)} %multiply_reduce_fusion.6, bf16[4,512,128]{2,1,0:T(8,128)(2,1)} %get-tuple-element.132, s32[]{:T(128)S(6)} %copy.12), kind=kOutput, calls=%fused_computation.clone.1 | convolution fusion | flops 1094713344 | bytes 10651652 | tf_op jit(solution)/shard_map/while/body/eval_jaxpr/dot_general | solution.py:12
  234.8 11.9 %convolution_add_fusion.2 = f32[64,8192]{1,0:T(8,128)S(1)} fusion(bf16[512,8192]{1,0:T(8,128)(2,1)} %exponential_convert_fusion.2, f32[64,8192]{1,0:T(8,128)S(1)} %get-tuple-element.123, pred[]{:T(512)S(6)} %compare.3, bf16[64,8192]{1,0:T(8,128)(2,1)S(1)} %copy-done), kind=kOutput, calls=%fused_computation.1.clone.1 | convolution fusion | flops 1074823168 | bytes 13631489 | tf_op jit(solution)/shard_map/while/body/eval_jaxpr/dot_general | solution.py:51
  247.7 9.0 %exponential_convert_fusion.2 = bf16[512,8192]{1,0:T(8,128)(2,1)} fusion(bf16[8192,128]{1,0:T(8,128)(2,1)} %get-tuple-element.134, f32[8192]{0:T(1024)S(1)} %get-tuple-element.133, f32[512]{0:T(512)S(1)} %multiply_reduce_fusion.6, bf16[4,512,128]{2,1,0:T(8,128)(2,1)} %get-tuple-element.132, s32[]{:T(128)S(6)} %copy.12), kind=kOutput, calls=%fused_computation.clone.1 | convolution fusion | flops 1094713344 | bytes 10651652 | tf_op jit(solution)/shard_map/while/body/eval_jaxpr/dot_general | solution.py:12
  256.7 11.9 %convolution_add_fusion.2 = f32[64,8192]{1,0:T(8,128)S(1)} fusion(bf16[512,8192]{1,0:T(8,128)(2,1)} %exponential_convert_fusion.2, f32[64,8192]{1,0:T(8,128)S(1)} %get-tuple-element.123, pred[]{:T(512)S(6)} %compare.3, bf16[64,8192]{1,0:T(8,128)(2,1)S(1)} %copy-done), kind=kOutput, calls=%fused_computation.1.clone.1 | convolution fusion | flops 1074823168 | bytes 13631489 | tf_op jit(solution)/shard_map/while/body/eval_jaxpr/dot_general | solution.py:51
  269.7 9.0 %exponential_convert_fusion.2 = bf16[512,8192]{1,0:T(8,128)(2,1)} fusion(bf16[8192,128]{1,0:T(8,128)(2,1)} %get-tuple-element.134, f32[8192]{0:T(1024)S(1)} %get-tuple-element.133, f32[512]{0:T(512)S(1)} %multiply_reduce_fusion.6, bf16[4,512,128]{2,1,0:T(8,128)(2,1)} %get-tuple-element.132, s32[]{:T(128)S(6)} %copy.12), kind=kOutput, calls=%fused_computation.clone.1 | convolution fusion | flops 1094713344 | bytes 10651652 | tf_op jit(solution)/shard_map/while/body/eval_jaxpr/dot_general | solution.py:12
  278.7 11.9 %convolution_add_fusion.2 = f32[64,8192]{1,0:T(8,128)S(1)} fusion(bf16[512,8192]{1,0:T(8,128)(2,1)} %exponential_convert_fusion.2, f32[64,8192]{1,0:T(8,128)S(1)} %get-tuple-element.123, pred[]{:T(512)S(6)} %compare.3, bf16[64,8192]{1,0:T(8,128)(2,1)S(1)} %copy-done), kind=kOutput, calls=%fused_computation.1.clone.1 | convolution fusion | flops 1074823168 | bytes 13631489 | tf_op jit(solution)/shard_map/while/body/eval_jaxpr/dot_general | solution.py:51
  290.6 85.9 %all-reduce.2 = bf16[64,8192]{1,0:T(8,128)(2,1)S(1)} all-reduce(f32[64,8192]{1,0:T(8,128)S(1)} %get-tuple-element.35), channel_id=1, replica_groups=mesh['grp'=8,'row'=32] {'grp','row'}, use_global_device_ids=true, to_apply=%region_6.7 | all-reduce | flops 524288 | bytes 3145728 | tf_op jit(solution)/shard_map/psum | solution.py:56
  376.5 4.4 fusion.3
  380.9 139.3 %reduce-scatter.3.cloned.1.call-done = f32[64,256]{1,0:T(8,128)} async-done(((f32[64,8192]{1,0:T(8,128)}), f32[64,256]{1,0:T(8,128)}) %reduce-scatter.3.cloned.1.call-update) | async-done | bytes 65552 | tf_op jit(solution)/shard_map/reduce_scatter | solution.py:62
  520.3 4.5 fusion.4
  524.9 144.8 %reduce-scatter.5.cloned.1.call-done = f32[64,256]{1,0:T(8,128)} async-done(((f32[64,8192]{1,0:T(8,128)}), f32[64,256]{1,0:T(8,128)}) %reduce-scatter.5.cloned.1.call-update) | async-done | bytes 65552 | tf_op jit(solution)/shard_map/reduce_scatter | solution.py:67
  670.7 72.6 %all-reduce = (f32[64]{0:T(128)S(1)}, f32[64]{0:T(128)S(1)}) all-reduce(f32[64]{0:T(128)S(1)} %multiply_reduce_fusion.4, f32[64]{0:T(128)S(1)} %multiply_reduce_fusion.3), channel_id=1, replica_groups=mesh['grp'=8,'row'=32] {'row'}, use_global_device_ids=true, to_apply=%region_1.2 | all-reduce | flops 128 | bytes 1024 | tf_op jit(solution)/shard_map/psum | solution.py:68
  744.3 67.9 %psum.31 = f32[64]{0:T(128)S(1)} all-reduce(f32[64]{0:T(128)S(1)} %get-tuple-element.71), channel_id=1, replica_groups=mesh['grp'=8,'row'=32] {'row'}, use_global_device_ids=true, to_apply=%region_12.13 | all-reduce | flops 64 | bytes 512 | tf_op jit(solution)/shard_map/psum | solution.py:72
  (36 shorter events, 6.5 us)
Async XLA Ops:
  7.2 67.6 %all-gather.4.cloned.1.call-start = ((), (), s32[]{:S(2)}) async-start(), calls=%async_computation.2 | async-start | bytes 1081344 | tf_op jit(solution)/shard_map/all_gather | solution.py:26
  8.7 130.0 %all-gather.6.cloned.1.call-start = ((), (), s32[]{:S(2)}) async-start(), calls=%async_computation.3 | async-start | bytes 1081344 | tf_op jit(solution)/shard_map/all_gather | solution.py:34
  79.3 123.4 %all-gather.8.cloned.1.call-start = ((), (), s32[]{:S(2)}) async-start(), calls=%async_computation.4 | async-start | bytes 1081344 | tf_op jit(solution)/shard_map/all_gather | solution.py:39
  143.3 377.0 %reduce-scatter.3.cloned.1.call-start = ((), (), s32[]{:S(2)}) async-start(), calls=%async_computation.5 | async-start | bytes 2162688 | tf_op jit(solution)/shard_map/reduce_scatter | solution.py:62
  203.7 9.1 %copy-start = (bf16[64,8192]{1,0:T(8,128)(2,1)S(1)}, bf16[64,8192]{1,0:T(8,128)(2,1)}, u32[]{:S(2)}) copy-start(bf16[64,8192]{1,0:T(8,128)(2,1)} %get-tuple-element.135) | copy-start | bytes 3145732 | tf_op jit(solution)/shard_map/while
  225.7 9.1 %copy-start = (bf16[64,8192]{1,0:T(8,128)(2,1)S(1)}, bf16[64,8192]{1,0:T(8,128)(2,1)}, u32[]{:S(2)}) copy-start(bf16[64,8192]{1,0:T(8,128)(2,1)} %get-tuple-element.135) | copy-start | bytes 3145732 | tf_op jit(solution)/shard_map/while
  247.7 9.1 %copy-start = (bf16[64,8192]{1,0:T(8,128)(2,1)S(1)}, bf16[64,8192]{1,0:T(8,128)(2,1)}, u32[]{:S(2)}) copy-start(bf16[64,8192]{1,0:T(8,128)(2,1)} %get-tuple-element.135) | copy-start | bytes 3145732 | tf_op jit(solution)/shard_map/while
  269.7 9.1 %copy-start = (bf16[64,8192]{1,0:T(8,128)(2,1)S(1)}, bf16[64,8192]{1,0:T(8,128)(2,1)}, u32[]{:S(2)}) copy-start(bf16[64,8192]{1,0:T(8,128)(2,1)} %get-tuple-element.135) | copy-start | bytes 3145732 | tf_op jit(solution)/shard_map/while
  380.9 288.8 %reduce-scatter.5.cloned.1.call-start = ((), (), s32[]{:S(2)}) async-start(), calls=%async_computation.6 | async-start | bytes 2162688 | tf_op jit(solution)/shard_map/reduce_scatter | solution.py:67
  520.3 4.5 copy-start.3
  520.3 149.4 %copy-start.1 = (f32[64,256]{1,0:T(8,128)S(1)}, f32[64,256]{1,0:T(8,128)}, u32[]{:S(2)}) copy-start(f32[64,256]{1,0:T(8,128)} %param.15) | copy-start | bytes 196612
  520.3 291.8 %copy-start.4 = (f32[64,256]{1,0:T(8,128)S(1)}, f32[64,256]{1,0:T(8,128)}, u32[]{:S(2)}) copy-start(f32[64,256]{1,0:T(8,128)} %param.13) | copy-start | bytes 196612
  744.3 68.6 %copy-start.2 = (f32[64,256]{1,0:T(8,128)}, f32[64,256]{1,0:T(8,128)S(1)}, u32[]{:S(2)}) copy-start(f32[64,256]{1,0:T(8,128)S(1)} %get-tuple-element.72) | copy-start | bytes 196612
Sparse Core Ops, SparseCore 0:
  10.3 64.4 all-gather.3
  79.4 59.2 all-gather.5
  143.4 59.2 all-gather.7
  381.0 139.2 reduce-scatter.2
  524.9 144.7 reduce-scatter.4
where the time goes:
time: 820 us; the launch traced here: 819 us
  waiting for transfers between devices  466 us (57%)
  blocking collectives  226 us (28%)
  matrix products  101 us (12%)
  between operations  13.8 us (2%)
  other arithmetic  11.2 us (1%)
    reduce_scatter x1, waiting for transfers between devices, local(): lax.psum_scatter(inner_terms, 'row', scatter_dimension=1, tiled=True)  145 us
    reduce_scatter x1, waiting for transfers between devices, local(): lax.psum_scatter(outer_terms, 'row', scatter_dimension=1, tiled=True)  139 us
    psum x1, blocking collectives, local(): summed_all = lax.psum(partial_sums, ('grp', 'row'))  85.9 us
    psum x1, blocking collectives, local(): old_norm = lax.psum(jnp.sum(residual * residual, axis=1), 'row')  72.6 us
    psum x1, blocking collectives, local(): new_norm = lax.psum(jnp.sum(next_residual * next_residual, axis=1), 'row')  67.9 us
    all_gather x1, waiting for transfers between devices, local(): lax.all_gather(direction_half, 'row', axis=1, tiled=True)  66 us
    all_gather x1, waiting for transfers between devices, local(): lax.all_gather(inner_half, 'row', axis=1, tiled=True)  59.4 us
    all_gather x1, waiting for transfers between devices, local(): lax.all_gather(outer_rows.astype(jnp.bfloat16), 'row', axis=1, tiled=True)  56.4 us
  transfers between devices with their start and end apart: 5, of which 5 were waited for; matrix products, arithmetic and copies ran while one was open for 0% of the time, Pallas kernels for 0%

commit v1 on v0

--- a/solution.py
+++ b/solution.py
@@ -53,7 +53,8 @@
     partial_sums, _ = lax.scan(
         one_block, jnp.zeros((targets, centers.shape[0]), jnp.float32), point_blocks
     )
-    summed_all = lax.psum(partial_sums, ("grp", "row"))
+    half = lax.psum(partial_sums, "grp")
+    summed_all = lax.psum(half, "row")
     own_normal = lax.dynamic_slice_in_dim(summed_all, lax.axis_index("row") * own_rows, own_rows, 1)
     normal_half = own_normal.astype(jnp.bfloat16)
     point_count = local_points * lax.axis_size("grp") * lax.axis_size("row")

time: 820 us -> 1020 us (1.24)
  waiting for transfers between devices: 466 us -> 604 us
  blocking collectives: 226 us -> 291 us
    psum x0 -> x1, waiting for transfers between devices: none -> 129 us  [local(): half = lax.psum(partial_sums, 'grp')]
    psum x1, blocking collectives: 85.9 us -> 150 us  [local(): summed_all = lax.psum(half, 'row')]
  transfers between devices with their start and end apart: 5 -> 6, of which waited for: 5 -> 6; matrix products, arithmetic and copies ran while one was open for 0% -> 0% of each run, Pallas kernels for 0% -> 0%
where the time goes in v1:
time: 1020 us
  waiting for transfers between devices  604 us (59%)
  blocking collectives  291 us (29%)
  matrix products  101 us (10%)
  between operations  14.2 us (1%)
  other arithmetic  11.2 us (1%)
    psum x1, blocking collectives, local(): summed_all = lax.psum(half, 'row')  150 us
    reduce_scatter x1, waiting for transfers between devices, local(): lax.psum_scatter(outer_terms, 'row', scatter_dimension=1, tiled=True)  148 us
    reduce_scatter x1, waiting for transfers between devices, local(): lax.psum_scatter(inner_terms, 'row', scatter_dimension=1, tiled=True)  145 us
    psum x1, waiting for transfers between devices, local(): half = lax.psum(partial_sums, 'grp')  129 us
    psum x1, blocking collectives, local(): old_norm = lax.psum(jnp.sum(residual * residual, axis=1), 'row')  72.6 us
    psum x1, blocking collectives, local(): new_norm = lax.psum(jnp.sum(next_residual * next_residual, axis=1), 'row')  67.9 us
    all_gather x1, waiting for transfers between devices, local(): lax.all_gather(direction_half, 'row', axis=1, tiled=True)  66 us
    all_gather x1, waiting for transfers between devices, local(): lax.all_gather(inner_half, 'row', axis=1, tiled=True)  59.4 us
  transfers between devices with their start and end apart: 6, of which 6 were waited for; matrix products, arithmetic and copies ran while one was open for 0% of the time, Pallas kernels for 0%

profile of v1, /device:TPU:1, one launch (start us, length us, event | category | flops | bytes accessed | tf_op | source)
XLA Modules:
  0.0 1023.1 jit_solution(1360982733832563381)
XLA Ops:
  7.2 1.5 convert_element_type.29
  8.7 66.0 %all-gather.4.cloned.1.call-done = bf16[64,8192]{1,0:T(8,128)(2,1)} async-done(((bf16[64,256]{1,0:T(8,128)(2,1)}), bf16[64,8192]{1,0:T(8,128)(2,1)}) %all-gather.4.cloned.1.call-update) | async-done | bytes 1048592 | tf_op jit(solution)/shard_map/all_gather | solution.py:26
  74.8 4.5 fusion.10
  79.4 59.4 %all-gather.6.cloned.1.call-done = bf16[64,8192]{1,0:T(8,128)(2,1)} async-done(((bf16[64,256]{1,0:T(8,128)(2,1)}), bf16[64,8192]{1,0:T(8,128)(2,1)}) %all-gather.6.cloned.1.call-update) | async-done | bytes 1048592 | tf_op jit(solution)/shard_map/all_gather | solution.py:34
  138.7 4.5 convolution_convert_fusion.1
  143.3 2.7 multiply_reduce_fusion.1
  146.1 56.6 %all-gather.8.cloned.1.call-done = bf16[64,8192]{1,0:T(8,128)(2,1)} async-done(((bf16[64,256]{1,0:T(8,128)(2,1)}), bf16[64,8192]{1,0:T(8,128)(2,1)}) %all-gather.8.cloned.1.call-update) | async-done | bytes 1048592 | tf_op jit(solution)/shard_map/all_gather | solution.py:39
  202.7 87.9 %while.11 = (s32[]{:T(128)}, f32[64,8192]{1,0:T(8,128)S(1)}, bf16[4,512,128]{2,1,0:T(8,128)(2,1)}, f32[8192]{0:T(1024)S(1)}, bf16[8192,128]{1,0:T(8,128)(2,1)}, ...) while((s32[]{:T(128)}, f32[64,8192]{1,0:T(8,128)S(1)}, bf16[4,512,128]{2,1,0:T(8,128)(2,1)}, ...), condition=%wide.region_5.6_spmd.clone, body=%wide.region_3.0_spmd.clone.sunk | while | flops 2169732608 | bytes 28610700 | solution.py:53
  203.7 9.1 exponential_convert_fusion.2
  212.8 11.9 %convolution_add_fusion.2 = f32[64,8192]{1,0:T(8,128)S(1)} fusion(bf16[512,8192]{1,0:T(8,128)(2,1)} %exponential_convert_fusion.2, f32[64,8192]{1,0:T(8,128)S(1)} %get-tuple-element.123, pred[]{:T(512)S(6)} %compare.3, bf16[64,8192]{1,0:T(8,128)(2,1)S(1)} %copy-done.1), kind=kOutput, calls=%fused_computation.1.clone.1 | convolution fusion | flops 1074823168 | bytes 13631489 | tf_op jit(solution)/shard_map/while/body/eval_jaxpr/dot_general | solution.py:51
  225.7 9.0 exponential_convert_fusion.2
  234.8 11.9 %convolution_add_fusion.2 = f32[64,8192]{1,0:T(8,128)S(1)} fusion(bf16[512,8192]{1,0:T(8,128)(2,1)} %exponential_convert_fusion.2, f32[64,8192]{1,0:T(8,128)S(1)} %get-tuple-element.123, pred[]{:T(512)S(6)} %compare.3, bf16[64,8192]{1,0:T(8,128)(2,1)S(1)} %copy-done.1), kind=kOutput, calls=%fused_computation.1.clone.1 | convolution fusion | flops 1074823168 | bytes 13631489 | tf_op jit(solution)/shard_map/while/body/eval_jaxpr/dot_general | solution.py:51
  247.7 9.0 exponential_convert_fusion.2
  256.8 11.9 %convolution_add_fusion.2 = f32[64,8192]{1,0:T(8,128)S(1)} fusion(bf16[512,8192]{1,0:T(8,128)(2,1)} %exponential_convert_fusion.2, f32[64,8192]{1,0:T(8,128)S(1)} %get-tuple-element.123, pred[]{:T(512)S(6)} %compare.3, bf16[64,8192]{1,0:T(8,128)(2,1)S(1)} %copy-done.1), kind=kOutput, calls=%fused_computation.1.clone.1 | convolution fusion | flops 1074823168 | bytes 13631489 | tf_op jit(solution)/shard_map/while/body/eval_jaxpr/dot_general | solution.py:51
  269.7 9.0 exponential_convert_fusion.2
  278.7 11.9 %convolution_add_fusion.2 = f32[64,8192]{1,0:T(8,128)S(1)} fusion(bf16[512,8192]{1,0:T(8,128)(2,1)} %exponential_convert_fusion.2, f32[64,8192]{1,0:T(8,128)S(1)} %get-tuple-element.123, pred[]{:T(512)S(6)} %compare.3, bf16[64,8192]{1,0:T(8,128)(2,1)S(1)} %copy-done.1), kind=kOutput, calls=%fused_computation.1.clone.1 | convolution fusion | flops 1074823168 | bytes 13631489 | tf_op jit(solution)/shard_map/while/body/eval_jaxpr/dot_general | solution.py:51
  292.0 129.0 %all-reduce.4.cloned.1.call-done = f32[64,8192]{1,0:T(8,128)} async-done(((f32[64,8192]{1,0:T(8,128)}), f32[64,8192]{1,0:T(8,128)}) %all-reduce.4.cloned.1.call-update) | async-done | bytes 2097168 | tf_op jit(solution)/shard_map/psum | solution.py:56
  421.0 150.3 %all-reduce.5 = bf16[64,8192]{1,0:T(8,128)(2,1)S(1)} all-reduce(f32[64,8192]{1,0:T(8,128)} %all-reduce.4.cloned.1.call-done), channel_id=1, replica_groups=mesh['grp'=8,'row'=32] {'row'}, use_global_device_ids=true, to_apply=%region_7.8 | all-reduce | flops 524288 | bytes 3145728 | tf_op jit(solution)/shard_map/psum | solution.py:57
  571.3 4.4 fusion.3
  575.8 147.9 %reduce-scatter.3.cloned.1.call-done = f32[64,256]{1,0:T(8,128)} async-done(((f32[64,8192]{1,0:T(8,128)}), f32[64,256]{1,0:T(8,128)}) %reduce-scatter.3.cloned.1.call-update) | async-done | bytes 65552 | tf_op jit(solution)/shard_map/reduce_scatter | solution.py:63
  723.7 4.5 fusion.4
  728.3 144.8 %reduce-scatter.5.cloned.1.call-done = f32[64,256]{1,0:T(8,128)} async-done(((f32[64,8192]{1,0:T(8,128)}), f32[64,256]{1,0:T(8,128)}) %reduce-scatter.5.cloned.1.call-update) | async-done | bytes 65552 | tf_op jit(solution)/shard_map/reduce_scatter | solution.py:68
  874.0 72.6 %all-reduce = (f32[64]{0:T(128)S(1)}, f32[64]{0:T(128)S(1)}) all-reduce(f32[64]{0:T(128)S(1)} %multiply_reduce_fusion.4, f32[64]{0:T(128)S(1)} %multiply_reduce_fusion.3), channel_id=1, replica_groups=mesh['grp'=8,'row'=32] {'row'}, use_global_device_ids=true, to_apply=%region_1.2 | all-reduce | flops 128 | bytes 1024 | tf_op jit(solution)/shard_map/psum | solution.py:69
  947.6 67.9 %psum.39 = f32[64]{0:T(128)S(1)} all-reduce(f32[64]{0:T(128)S(1)} %get-tuple-element.71), channel_id=1, replica_groups=mesh['grp'=8,'row'=32] {'row'}, use_global_device_ids=true, to_apply=%region_13.14 | all-reduce | flops 64 | bytes 512 | tf_op jit(solution)/shard_map/psum | solution.py:73
  (41 shorter events, 8.7 us)
Async XLA Ops:
  7.2 67.6 %all-gather.4.cloned.1.call-start = ((), (), s32[]{:S(2)}) async-start(), calls=%async_computation.2 | async-start | bytes 1081344 | tf_op jit(solution)/shard_map/all_gather | solution.py:26
  8.7 130.0 %all-gather.6.cloned.1.call-start = ((), (), s32[]{:S(2)}) async-start(), calls=%async_computation.3 | async-start | bytes 1081344 | tf_op jit(solution)/shard_map/all_gather | solution.py:34
  79.3 123.4 %all-gather.8.cloned.1.call-start = ((), (), s32[]{:S(2)}) async-start(), calls=%async_computation.4 | async-start | bytes 1081344 | tf_op jit(solution)/shard_map/all_gather | solution.py:39
  143.3 277.8 %all-reduce.4.cloned.1.call-start = ((), (), s32[]{:S(2)}) async-start(), calls=%async_computation.5 | async-start | bytes 4194304 | tf_op jit(solution)/shard_map/psum | solution.py:56
  203.7 9.1 copy-start.1
  225.7 9.1 copy-start.1
  247.7 9.1 copy-start.1
  269.7 9.1 copy-start.1
  290.6 1.3 copy-start
  291.9 431.7 %reduce-scatter.3.cloned.1.call-start = ((), (), s32[]{:S(2)}) async-start(), calls=%async_computation.6 | async-start | bytes 2162688 | tf_op jit(solution)/shard_map/reduce_scatter | solution.py:63
  575.8 297.3 %reduce-scatter.5.cloned.1.call-start = ((), (), s32[]{:S(2)}) async-start(), calls=%async_computation.7 | async-start | bytes 2162688 | tf_op jit(solution)/shard_map/reduce_scatter | solution.py:68
  723.7 4.5 copy-start.4
  723.7 149.4 %copy-start.2 = (f32[64,256]{1,0:T(8,128)S(1)}, f32[64,256]{1,0:T(8,128)}, u32[]{:S(2)}) copy-start(f32[64,256]{1,0:T(8,128)} %param.15) | copy-start | bytes 196612
  723.7 291.8 %copy-start.5 = (f32[64,256]{1,0:T(8,128)S(1)}, f32[64,256]{1,0:T(8,128)}, u32[]{:S(2)}) copy-start(f32[64,256]{1,0:T(8,128)} %param.13) | copy-start | bytes 196612
  947.6 68.6 %copy-start.3 = (f32[64,256]{1,0:T(8,128)}, f32[64,256]{1,0:T(8,128)S(1)}, u32[]{:S(2)}) copy-start(f32[64,256]{1,0:T(8,128)S(1)} %get-tuple-element.72) | copy-start | bytes 196612
Sparse Core Ops, SparseCore 0:
  10.3 64.4 all-gather.3
  79.4 59.2 all-gather.5
  143.4 59.2 all-gather.7
  292.1 128.9 all-reduce.3
  575.9 147.7 reduce-scatter.2
  728.3 144.7 reduce-scatter.4
